TPU v7x, 32 devices: a whole 2x2x4 slice. The times are simulated.
32 devices in a mesh: ma: 16 (over z, y, core), freq: 2 (over x).
Axes of the slice: x: 2, y: 2, z: 4, core: 2. Of those that a mesh axis runs over, the one named last changes fastest.
Arguments:
- right_side: float32 [128, 8, 2, 512], P('ma', 'freq'), may hold values from -60 to 60
- start_field: float32 [128, 8, 2, 512], P('ma', 'freq'), may hold values from -6 to 6
- beam: float32 [128, 8, 2, 16, 512], P('ma', 'freq'), may hold values from -0.75 to 0.75
- noise: float32 [128, 8, 16], P('ma', 'freq'), may hold values from 0.3 to 3
- inv_power: float32 [512], replicated, may hold values from 0.5 to 2
- smooth: float32 [512], replicated, may hold values from 0.5 to 4
Outputs:
- solution_field: float32 [128, 8, 2, 512], P('ma', 'freq')
- residual: float32 [128, 8, 2, 512], P('ma', 'freq')
All inputs are finite; a program needn't handle non-finite values.
Results may differ from a plain program's by a relative error of at most 0.0003.
Values sent between devices are 32-bit elements; how exact they have to be, the bound alone decides.
A program may use at most 64 MiB of HBM per device.

v0:
```python
import jax
import jax.numpy as jnp
from jax import lax
from jax.sharding import PartitionSpec as P

ITERS = 2


def extended(array, sides, width):
    for axis, dim in sides:
        size, length = (lax.axis_size(axis), array.shape[dim])
        up = [(i, (i + 1) % size) for i in range(size - 1)]
        down = [(j, i) for i, j in up]
        last = lax.slice_in_dim(array, length - width, length, axis=dim)
        leading = lax.slice_in_dim(array, 0, width, axis=dim)
        before = lax.ppermute(last, axis, up)
        after = lax.ppermute(leading, axis, down)
        array = jnp.concatenate([before, array, after], axis=dim)
    return array


def beam_image(field, beam, noise):
    projected = jnp.einsum("mfakl,mfbl->mfabk", beam, field, precision=lax.Precision.HIGHEST)
    real_part = projected[:, :, 0, 0] + projected[:, :, 1, 1]
    imaginary = projected[:, :, 0, 1] - projected[:, :, 1, 0]
    weighted = jnp.stack([real_part, imaginary], axis=2) * noise[:, :, None, :]
    back = jnp.einsum("mfakl,mfbk->mfabl", beam, weighted, precision=lax.Precision.HIGHEST)
    return jnp.stack(
        [back[:, :, 0, 0] - back[:, :, 1, 1], back[:, :, 0, 1] + back[:, :, 1, 0]], axis=2
    )


def prior_term(padded, field, first, total, smooth):
    channel = first + jnp.arange(field.shape[1], dtype=jnp.int32)
    weight = (channel > 0).astype(jnp.float32) + (channel < total - 1).astype(jnp.float32)
    return smooth * (weight[None, :, None, None] * field - padded[:, :-2] - padded[:, 2:])


def two_products(vector, applied):
    return lax.psum((jnp.sum(vector * vector), jnp.sum(vector * applied)), ("ma", "freq"))


def shards(right_side, start_field, beam, noise, inv_power, smooth):
    first = lax.axis_index("freq") * right_side.shape[1]
    total = right_side.shape[1] * lax.axis_size("freq")

    def padded_of(field):
        return extended(field, (("freq", 1),), 1)

    def operate(field):
        prior = prior_term(padded_of(field), field, first, total, smooth)
        return beam_image(field, beam, noise) + inv_power * field + prior

    solution = start_field
    resid_now = right_side - operate(start_field)
    applied = operate(resid_now)
    norm_now, curve_now = two_products(resid_now, applied)
    step_size = norm_now / curve_now
    direction = resid_now
    along = applied
    for turn in range(ITERS):
        solution = solution + step_size * direction
        resid_now = resid_now - step_size * along
        if turn + 1 < ITERS:
            applied = operate(resid_now)
            norm_next, curve_now = two_products(resid_now, applied)
            growth = norm_next / norm_now
            step_size = norm_next / (curve_now - growth * norm_next / step_size)
            direction = resid_now + growth * direction
            along = applied + growth * along
            norm_now = norm_next
    return (solution, resid_now)


def solution(mesh):
    in_specs = (
        P("ma", "freq", None, None),
        P("ma", "freq", None, None),
        P("ma", "freq", None, None, None),
        P("ma", "freq", None),
        P(),
        P(),
    )
    out_specs = (P("ma", "freq", None, None), P("ma", "freq", None, None))
    return jax.shard_map(shards, mesh=mesh, in_specs=in_specs, out_specs=out_specs, check_vma=False)
```

profile of v0, /device:TPU:0, one launch (start us, length us, event | category | flops | bytes accessed | tf_op | source)
XLA Modules:
  0.0 144.0 jit_solution(10948142598104500641)
XLA Ops:
  0.6 0.0 copy-start
  0.7 0.9 fusion.42
  1.6 4.9 %collective-permute-start = (f32[8,1,2,512]{3,2,1,0:T(2,128)S(1)}, f32[8,1,2,512]{3,2,1,0:T(2,128)S(1)}, u32[]{:S(2)}, u32[]{:S(2)}) collective-permute-start(f32[8,1,2,512]{3,2,1,0:T(2,128)S(1)} %get-tuple-element.22), channel_id=1, source_target_pairs={{0,1},{2,3},{4,5},{6,7},{8,9},{10,11},{12,13},{14,15},{16,17},{18,... | collective-permute-start | bytes 98312 | tf_op jit(solution)/shard_map/ppermute | solution.py:16
  6.5 1.3 collective-permute-start.1
  7.8 8.3 %convolution_bitcast_fusion.1 = f32[8,4,2,2,16]{4,3,2,1,0:T(2,128)S(1)} fusion(f32[8,4,2,16,512]{4,3,2,1,0:T(8,128)S(1)} %copy-done, f32[8,4,2,512]{3,2,1,0:T(2,128)} %param.7), kind=kOutput, calls=%fused_computation.1 | convolution fusion | flops 12582912 | bytes 2236416 | tf_op jit(solution)/shard_map/mfakl,mfbl->mfabk/dot_general | solution.py:23
  16.1 0.0 copy-start.4
  16.1 0.0 copy-start.5
  16.2 1.1 convolution_bitcast_fusion
  17.3 0.1 fusion.22
  17.4 0.1 fusion.24
  17.6 0.3 fusion.11
  17.9 7.4 %fusion.15 = f32[8,4,2,2,16]{4,2,3,1,0:T(2,128)S(1)} fusion(f32[8,4,2,16,512]{4,3,2,1,0:T(8,128)S(1)} %copy-done, f32[8,4,2,512]{3,2,1,0:T(2,128)S(1)} %fusion.11), kind=kOutput, calls=%fused_computation.28 | convolution fusion | flops 12582912 | bytes 2236416 | tf_op jit(solution)/shard_map/mfakl,mfbl->mfabk/dot_general | solution.py:23
  25.4 1.3 fusion.30
  26.7 0.1 copy.46
  26.9 4.5 %collective-permute-start.2 = (f32[8,1,2,512]{3,2,1,0:T(2,128)S(1)}, f32[8,1,2,512]{3,2,1,0:T(2,128)S(1)}, u32[]{:S(2)}, u32[]{:S(2)}) collective-permute-start(f32[8,1,2,512]{3,2,1,0:T(2,128)S(1)} %get-tuple-element.20), channel_id=1, source_target_pairs={{0,1},{2,3},{4,5},{6,7},{8,9},{10,11},{12,13},{14,15},{16,17},{18,... | collective-permute-start | bytes 98312 | tf_op jit(solution)/shard_map/ppermute | solution.py:16
  31.4 1.3 collective-permute-start.3
  32.7 0.1 fusion.21
  32.9 0.1 collective-permute-done.2
  33.0 4.2 %collective-permute-done.3 = f32[8,1,2,512]{3,2,1,0:T(2,128)S(1)} collective-permute-done((f32[8,1,2,512]{3,2,1,0:T(2,128)S(1)}, f32[8,1,2,512]{3,2,1,0:T(2,128)S(1)}, u32[]{:S(2)}, u32[]{:S(2)}) %collective-permute-start.3) | collective-permute-done | bytes 32800 | tf_op jit(solution)/shard_map/ppermute | solution.py:17
  37.2 1.1 multiply_reduce_fusion.2
  38.3 39.8 %all-reduce.1 = (f32[]{:T(128)}, f32[]{:T(128)}) all-reduce(f32[]{:T(128)} %get-tuple-element.5, f32[]{:T(128)} %get-tuple-element.4), channel_id=1, replica_groups=mesh['ma'=16,'freq'=2] {'ma','freq'}, use_global_device_ids=true, to_apply=%region_1.0 | all-reduce | flops 2 | bytes 16 | tf_op jit(solution)/shard_map/psum | solution.py:40
  79.4 7.4 %fusion.13 = f32[8,4,2,2,16]{4,2,3,1,0:T(2,128)S(1)} fusion(f32[8,4,2,16,512]{4,3,2,1,0:T(8,128)S(1)} %copy-done, f32[8,4,2,512]{3,2,1,0:T(2,128)S(1)} %bitcast.90), kind=kOutput, calls=%fused_computation.26 | convolution fusion | flops 12582912 | bytes 2236416 | tf_op jit(solution)/shard_map/mfakl,mfbl->mfabk/dot_general | solution.py:23
  86.9 1.1 fusion.28
  88.0 0.1 copy.45
  88.2 4.2 %collective-permute-start.4 = (f32[8,1,2,512]{3,2,1,0:T(2,128)S(1)}, f32[8,1,2,512]{3,2,1,0:T(2,128)S(1)}, u32[]{:S(2)}, u32[]{:S(2)}) collective-permute-start(f32[8,1,2,512]{3,2,1,0:T(2,128)S(1)} %get-tuple-element.18), channel_id=1, source_target_pairs={{0,1},{2,3},{4,5},{6,7},{8,9},{10,11},{12,13},{14,15},{16,17},{18,... | collective-permute-start | bytes 98312 | tf_op jit(solution)/shard_map/ppermute | solution.py:16
  92.4 1.3 collective-permute-start.5
  93.7 0.1 fusion.19
  93.8 0.1 collective-permute-done.4
  93.9 4.2 %collective-permute-done.5 = f32[8,1,2,512]{3,2,1,0:T(2,128)S(1)} collective-permute-done((f32[8,1,2,512]{3,2,1,0:T(2,128)S(1)}, f32[8,1,2,512]{3,2,1,0:T(2,128)S(1)}, u32[]{:S(2)}, u32[]{:S(2)}) %collective-permute-start.5) | collective-permute-done | bytes 32800 | tf_op jit(solution)/shard_map/ppermute | solution.py:17
  98.2 1.1 multiply_reduce_fusion
  99.3 39.4 %all-reduce = (f32[]{:T(128)}, f32[]{:T(128)}) all-reduce(f32[]{:T(128)} %get-tuple-element.3, f32[]{:T(128)} %get-tuple-element.2), channel_id=1, replica_groups=mesh['ma'=16,'freq'=2] {'ma','freq'}, use_global_device_ids=true, to_apply=%region_5.0 | all-reduce | flops 2 | bytes 16 | tf_op jit(solution)/shard_map/psum | solution.py:40
  143.3 0.8 multiply_subtract_fusion
  (24 shorter events, 0.2 us)
Async XLA Ops:
  0.6 7.1 %copy-start = (f32[8,4,2,16,512]{4,3,2,1,0:T(8,128)S(1)}, f32[8,4,2,16,512]{4,3,2,1,0:T(8,128)}, u32[]{:S(2)}) copy-start(f32[8,4,2,16,512]{4,3,2,1,0:T(8,128)} %param.8) | copy-start | bytes 6291460
  0.6 15.5 %copy-start.2 = (f32[8,4,16]{2,1,0:T(4,128)S(1)}, f32[8,4,16]{2,1,0:T(4,128)}, u32[]{:S(2)}) copy-start(f32[8,4,16]{2,1,0:T(4,128)} %param.9) | copy-start | bytes 6148
  1.6 16.0 %collective-permute-start = (f32[8,1,2,512]{3,2,1,0:T(2,128)S(1)}, f32[8,1,2,512]{3,2,1,0:T(2,128)S(1)}, u32[]{:S(2)}, u32[]{:S(2)}) collective-permute-start(f32[8,1,2,512]{3,2,1,0:T(2,128)S(1)} %get-tuple-element.22), channel_id=1, source_target_pairs={{0,1},{2,3},{4,5},{6,7},{8,9},{10,11},{12,13},{14,15},{16,17},{18,... | collective-permute-start | bytes 98312 | tf_op jit(solution)/shard_map/ppermute | solution.py:16
  6.5 11.1 %collective-permute-start.1 = (f32[8,1,2,512]{3,2,1,0:T(2,128)S(1)}, f32[8,1,2,512]{3,2,1,0:T(2,128)S(1)}, u32[]{:S(2)}, u32[]{:S(2)}) collective-permute-start(f32[8,1,2,512]{3,2,1,0:T(2,128)S(1)} %get-tuple-element.23), channel_id=1, source_target_pairs={{1,0},{3,2},{5,4},{7,6},{9,8},{11,10},{13,12},{15,14},{17,16},{19,... | collective-permute-start | bytes 98312 | tf_op jit(solution)/shard_map/ppermute | solution.py:17
  16.1 1.5 %copy-start.1 = (f32[8,4,2,512]{3,2,1,0:T(2,128)S(1)}, f32[8,4,2,512]{3,2,1,0:T(2,128)}, u32[]{:S(2)}) copy-start(f32[8,4,2,512]{3,2,1,0:T(2,128)} %param.7) | copy-start | bytes 393220
  16.1 1.5 %copy-start.3 = (f32[8,4,2,512]{3,2,1,0:T(2,128)S(1)}, f32[8,4,2,512]{3,2,1,0:T(2,128)}, u32[]{:S(2)}) copy-start(f32[8,4,2,512]{3,2,1,0:T(2,128)} %param.6) | copy-start | bytes 393220
  16.1 1.6 %copy-start.4 = (f32[512]{0:T(512)S(1)}, f32[512]{0:T(512)}, u32[]{:S(2)}) copy-start(f32[512]{0:T(512)} %param.11) | copy-start | bytes 6148
  16.1 1.5 %copy-start.5 = (f32[512]{0:T(512)S(1)}, f32[512]{0:T(512)}, u32[]{:S(2)}) copy-start(f32[512]{0:T(512)} %param.10) | copy-start | bytes 6148
  26.9 6.1 %collective-permute-start.2 = (f32[8,1,2,512]{3,2,1,0:T(2,128)S(1)}, f32[8,1,2,512]{3,2,1,0:T(2,128)S(1)}, u32[]{:S(2)}, u32[]{:S(2)}) collective-permute-start(f32[8,1,2,512]{3,2,1,0:T(2,128)S(1)} %get-tuple-element.20), channel_id=1, source_target_pairs={{0,1},{2,3},{4,5},{6,7},{8,9},{10,11},{12,13},{14,15},{16,17},{18,... | collective-permute-start | bytes 98312 | tf_op jit(solution)/shard_map/ppermute | solution.py:16
  31.4 5.8 %collective-permute-start.3 = (f32[8,1,2,512]{3,2,1,0:T(2,128)S(1)}, f32[8,1,2,512]{3,2,1,0:T(2,128)S(1)}, u32[]{:S(2)}, u32[]{:S(2)}) collective-permute-start(f32[8,1,2,512]{3,2,1,0:T(2,128)S(1)} %get-tuple-element.21), channel_id=1, source_target_pairs={{1,0},{3,2},{5,4},{7,6},{9,8},{11,10},{13,12},{15,14},{17,16},{19,... | collective-permute-start | bytes 98312 | tf_op jit(solution)/shard_map/ppermute | solution.py:17
  88.2 5.8 %collective-permute-start.4 = (f32[8,1,2,512]{3,2,1,0:T(2,128)S(1)}, f32[8,1,2,512]{3,2,1,0:T(2,128)S(1)}, u32[]{:S(2)}, u32[]{:S(2)}) collective-permute-start(f32[8,1,2,512]{3,2,1,0:T(2,128)S(1)} %get-tuple-element.18), channel_id=1, source_target_pairs={{0,1},{2,3},{4,5},{6,7},{8,9},{10,11},{12,13},{14,15},{16,17},{18,... | collective-permute-start | bytes 98312 | tf_op jit(solution)/shard_map/ppermute | solution.py:16
  92.4 5.8 %collective-permute-start.5 = (f32[8,1,2,512]{3,2,1,0:T(2,128)S(1)}, f32[8,1,2,512]{3,2,1,0:T(2,128)S(1)}, u32[]{:S(2)}, u32[]{:S(2)}) collective-permute-start(f32[8,1,2,512]{3,2,1,0:T(2,128)S(1)} %get-tuple-element.19), channel_id=1, source_target_pairs={{1,0},{3,2},{5,4},{7,6},{9,8},{11,10},{13,12},{15,14},{17,16},{19,... | collective-permute-start | bytes 98312 | tf_op jit(solution)/shard_map/ppermute | solution.py:17
where the time goes:
time: 145 us; the launch traced here: 144 us
  blocking collectives  79.2 us (55%)
  matrix products  26.7 us (18%)
  starting transfers between devices  17.5 us (12%)
  waiting for transfers between devices  8.73 us (6%)
  between operations  6.85 us (5%)
  other arithmetic  3.86 us (3%)
    psum x2, blocking collectives, two_products(): lax.psum((jnp.sum(vector * vector), jnp.sum(vector * applied)), ('ma', 'f...  79.2 us
    dot_general x3, matrix products, beam_image(): jnp.einsum('mfakl,mfbl->mfabk', beam, field, precision=lax.Precision.HIGH...  23.1 us
    ppermute x3, starting transfers between devices, extended(): before = lax.ppermute(last, axis, up)  13.6 us
    ppermute x3, waiting for transfers between devices, extended(): after = lax.ppermute(leading, axis, down)  8.46 us
    ppermute x3, starting transfers between devices, extended(): after = lax.ppermute(leading, axis, down)  3.88 us
    dot_general x3, matrix products, beam_image(): jnp.einsum('mfakl,mfbk->mfabl', beam, weighted, precision=lax.Precision.H...  3.6 us
  transfers between devices with their start and end apart: 6, of which 4 were waited for; matrix products, arithmetic and copies ran while one was open for 7% of the time, Pallas kernels for 0%

commit v1 on v0

--- a/solution.py
+++ b/solution.py
@@ -37,7 +37,9 @@
 
 
 def two_products(vector, applied):
-    return lax.psum((jnp.sum(vector * vector), jnp.sum(vector * applied)), ("ma", "freq"))
+    return lax.psum(
+        lax.psum((jnp.sum(vector * vector), jnp.sum(vector * applied)), "freq"), axis_name="ma"
+    )
 
 
 def shards(right_side, start_field, beam, noise, inv_power, smooth):

time: 145 us -> 135 us (0.931)
  blocking collectives: 79.2 us -> 72.3 us
  starting transfers between devices: 17.5 us -> 15.5 us
    psum x2 -> x4, blocking collectives: 79.2 us -> 72.3 us  [the longest x2 61.1 us: two_products(): lax.psum(lax.psum((jnp.sum(vector * vector), jnp.sum(vector * applied)),...]
    ppermute x3, starting transfers between devices: 13.6 us -> 11.6 us  [extended(): before = lax.ppermute(last, axis, up)]
where the time goes in v1:
time: 135 us
  blocking collectives  72.3 us (54%)
  matrix products  26.7 us (20%)
  starting transfers between devices  15.5 us (11%)
  waiting for transfers between devices  8.73 us (6%)
  between operations  6.7 us (5%)
  other arithmetic  3.87 us (3%)
    psum x2, blocking collectives, two_products(): lax.psum(lax.psum((jnp.sum(vector * vector), jnp.sum(vector * applied)),...  61.1 us
    dot_general x3, matrix products, beam_image(): jnp.einsum('mfakl,mfbl->mfabk', beam, field, precision=lax.Precision.HIGH...  23.1 us
    ppermute x3, starting transfers between devices, extended(): before = lax.ppermute(last, axis, up)  11.6 us
    psum x2, blocking collectives, two_products(): lax.psum((jnp.sum(vector * vector), jnp.sum(vector * applied)), 'freq')  11.1 us
    ppermute x3, waiting for transfers between devices, extended(): after = lax.ppermute(leading, axis, down)  8.46 us
    ppermute x3, starting transfers between devices, extended(): after = lax.ppermute(leading, axis, down)  3.88 us
    dot_general x3, matrix products, beam_image(): jnp.einsum('mfakl,mfbk->mfabl', beam, weighted, precision=lax.Precision.H...  3.6 us
  transfers between devices with their start and end apart: 6, of which 4 were waited for; matrix products, arithmetic and copies ran while one was open for 7% of the time, Pallas kernels for 0%

profile of v1, /device:TPU:0, one launch (start us, length us, event | category | flops | bytes accessed | tf_op | source)
XLA Modules:
  0.0 135.0 jit_solution(6279468126549038329)
XLA Ops:
  0.7 0.9 fusion.42
  1.6 4.9 %collective-permute-start = (f32[8,1,2,512]{3,2,1,0:T(2,128)S(1)}, f32[8,1,2,512]{3,2,1,0:T(2,128)S(1)}, u32[]{:S(2)}, u32[]{:S(2)}) collective-permute-start(f32[8,1,2,512]{3,2,1,0:T(2,128)S(1)} %get-tuple-element.26), channel_id=1, source_target_pairs={{0,1},{2,3},{4,5},{6,7},{8,9},{10,11},{12,13},{14,15},{16,17},{18,... | collective-permute-start | bytes 98312 | tf_op jit(solution)/shard_map/ppermute | solution.py:16
  6.5 1.3 collective-permute-start.1
  7.8 8.3 %convolution_bitcast_fusion.1 = f32[8,4,2,2,16]{4,3,2,1,0:T(2,128)S(1)} fusion(f32[8,4,2,16,512]{4,3,2,1,0:T(8,128)S(1)} %copy-done, f32[8,4,2,512]{3,2,1,0:T(2,128)} %param.7), kind=kOutput, calls=%fused_computation.1 | convolution fusion | flops 12582912 | bytes 2236416 | tf_op jit(solution)/shard_map/mfakl,mfbl->mfabk/dot_general | solution.py:23
  16.1 0.0 copy-start.4
  16.2 1.1 convolution_bitcast_fusion
  17.3 0.1 fusion.22
  17.4 0.1 fusion.24
  17.6 0.3 fusion.11
  17.9 7.4 %fusion.15 = f32[8,4,2,2,16]{4,2,3,1,0:T(2,128)S(1)} fusion(f32[8,4,2,16,512]{4,3,2,1,0:T(8,128)S(1)} %copy-done, f32[8,4,2,512]{3,2,1,0:T(2,128)S(1)} %fusion.11), kind=kOutput, calls=%fused_computation.28 | convolution fusion | flops 12582912 | bytes 2236416 | tf_op jit(solution)/shard_map/mfakl,mfbl->mfabk/dot_general | solution.py:23
  25.4 1.3 fusion.30
  26.7 0.1 copy.46
  26.9 4.5 %collective-permute-start.2 = (f32[8,1,2,512]{3,2,1,0:T(2,128)S(1)}, f32[8,1,2,512]{3,2,1,0:T(2,128)S(1)}, u32[]{:S(2)}, u32[]{:S(2)}) collective-permute-start(f32[8,1,2,512]{3,2,1,0:T(2,128)S(1)} %get-tuple-element.24), channel_id=1, source_target_pairs={{0,1},{2,3},{4,5},{6,7},{8,9},{10,11},{12,13},{14,15},{16,17},{18,... | collective-permute-start | bytes 98312 | tf_op jit(solution)/shard_map/ppermute | solution.py:16
  31.4 1.3 collective-permute-start.3
  32.7 0.1 fusion.21
  32.9 0.1 collective-permute-done.2
  33.0 4.2 %collective-permute-done.3 = f32[8,1,2,512]{3,2,1,0:T(2,128)S(1)} collective-permute-done((f32[8,1,2,512]{3,2,1,0:T(2,128)S(1)}, f32[8,1,2,512]{3,2,1,0:T(2,128)S(1)}, u32[]{:S(2)}, u32[]{:S(2)}) %collective-permute-start.3) | collective-permute-done | bytes 32800 | tf_op jit(solution)/shard_map/ppermute | solution.py:17
  37.2 1.1 multiply_reduce_fusion.2
  38.3 5.5 %all-reduce.3 = (f32[]{:T(128)}, f32[]{:T(128)}) all-reduce(f32[]{:T(128)} %get-tuple-element.5, f32[]{:T(128)} %get-tuple-element.4), channel_id=1, replica_groups=mesh['ma'=16,'freq'=2] {'freq'}, use_global_device_ids=true, to_apply=%region_1.0 | all-reduce | flops 2 | bytes 16 | tf_op jit(solution)/shard_map/psum | solution.py:41
  43.8 30.9 %all-reduce.1 = (f32[]{:T(128)}, f32[]{:T(128)}) all-reduce(f32[]{:T(128)} %get-tuple-element.12, f32[]{:T(128)} %get-tuple-element.13), channel_id=1, replica_groups=mesh['ma'=16,'freq'=2] {'ma'}, use_global_device_ids=true, to_apply=%region_2.0 | all-reduce | flops 2 | bytes 16 | tf_op jit(solution)/shard_map/psum | solution.py:40
  76.2 7.4 %fusion.13 = f32[8,4,2,2,16]{4,2,3,1,0:T(2,128)S(1)} fusion(f32[8,4,2,16,512]{4,3,2,1,0:T(8,128)S(1)} %copy-done, f32[8,4,2,512]{3,2,1,0:T(2,128)S(1)} %bitcast.90), kind=kOutput, calls=%fused_computation.26 | convolution fusion | flops 12582912 | bytes 2236416 | tf_op jit(solution)/shard_map/mfakl,mfbl->mfabk/dot_general | solution.py:23
  83.6 1.1 fusion.28
  84.8 0.1 copy.45
  84.9 2.2 %collective-permute-start.4 = (f32[8,1,2,512]{3,2,1,0:T(2,128)S(1)}, f32[8,1,2,512]{3,2,1,0:T(2,128)S(1)}, u32[]{:S(2)}, u32[]{:S(2)}) collective-permute-start(f32[8,1,2,512]{3,2,1,0:T(2,128)S(1)} %get-tuple-element.22), channel_id=1, source_target_pairs={{0,1},{2,3},{4,5},{6,7},{8,9},{10,11},{12,13},{14,15},{16,17},{18,... | collective-permute-start | bytes 98312 | tf_op jit(solution)/shard_map/ppermute | solution.py:16
  87.1 1.3 collective-permute-start.5
  88.4 0.1 fusion.19
  88.6 0.1 collective-permute-done.4
  88.7 4.2 %collective-permute-done.5 = f32[8,1,2,512]{3,2,1,0:T(2,128)S(1)} collective-permute-done((f32[8,1,2,512]{3,2,1,0:T(2,128)S(1)}, f32[8,1,2,512]{3,2,1,0:T(2,128)S(1)}, u32[]{:S(2)}, u32[]{:S(2)}) %collective-permute-start.5) | collective-permute-done | bytes 32800 | tf_op jit(solution)/shard_map/ppermute | solution.py:17
  92.9 1.1 multiply_reduce_fusion
  94.1 5.6 %all-reduce.2 = (f32[]{:T(128)}, f32[]{:T(128)}) all-reduce(f32[]{:T(128)} %get-tuple-element.3, f32[]{:T(128)} %get-tuple-element.2), channel_id=1, replica_groups=mesh['ma'=16,'freq'=2] {'freq'}, use_global_device_ids=true, to_apply=%region_7.0 | all-reduce | flops 2 | bytes 16 | tf_op jit(solution)/shard_map/psum | solution.py:41
  99.6 30.2 %all-reduce = (f32[]{:T(128)}, f32[]{:T(128)}) all-reduce(f32[]{:T(128)} %get-tuple-element.10, f32[]{:T(128)} %get-tuple-element.11), channel_id=1, replica_groups=mesh['ma'=16,'freq'=2] {'ma'}, use_global_device_ids=true, to_apply=%region_8.0 | all-reduce | flops 2 | bytes 16 | tf_op jit(solution)/shard_map/psum | solution.py:40
  134.2 0.8 multiply_subtract_fusion
  (26 shorter events, 0.2 us)
Async XLA Ops:
  0.6 7.1 %copy-start = (f32[8,4,2,16,512]{4,3,2,1,0:T(8,128)S(1)}, f32[8,4,2,16,512]{4,3,2,1,0:T(8,128)}, u32[]{:S(2)}) copy-start(f32[8,4,2,16,512]{4,3,2,1,0:T(8,128)} %param.8) | copy-start | bytes 6291460
  0.6 15.5 %copy-start.2 = (f32[8,4,16]{2,1,0:T(4,128)S(1)}, f32[8,4,16]{2,1,0:T(4,128)}, u32[]{:S(2)}) copy-start(f32[8,4,16]{2,1,0:T(4,128)} %param.9) | copy-start | bytes 6148
  1.6 16.0 %collective-permute-start = (f32[8,1,2,512]{3,2,1,0:T(2,128)S(1)}, f32[8,1,2,512]{3,2,1,0:T(2,128)S(1)}, u32[]{:S(2)}, u32[]{:S(2)}) collective-permute-start(f32[8,1,2,512]{3,2,1,0:T(2,128)S(1)} %get-tuple-element.26), channel_id=1, source_target_pairs={{0,1},{2,3},{4,5},{6,7},{8,9},{10,11},{12,13},{14,15},{16,17},{18,... | collective-permute-start | bytes 98312 | tf_op jit(solution)/shard_map/ppermute | solution.py:16
  6.5 11.1 %collective-permute-start.1 = (f32[8,1,2,512]{3,2,1,0:T(2,128)S(1)}, f32[8,1,2,512]{3,2,1,0:T(2,128)S(1)}, u32[]{:S(2)}, u32[]{:S(2)}) collective-permute-start(f32[8,1,2,512]{3,2,1,0:T(2,128)S(1)} %get-tuple-element.27), channel_id=1, source_target_pairs={{1,0},{3,2},{5,4},{7,6},{9,8},{11,10},{13,12},{15,14},{17,16},{19,... | collective-permute-start | bytes 98312 | tf_op jit(solution)/shard_map/ppermute | solution.py:17
  16.1 1.5 %copy-start.1 = (f32[8,4,2,512]{3,2,1,0:T(2,128)S(1)}, f32[8,4,2,512]{3,2,1,0:T(2,128)}, u32[]{:S(2)}) copy-start(f32[8,4,2,512]{3,2,1,0:T(2,128)} %param.7) | copy-start | bytes 393220
  16.1 1.5 %copy-start.3 = (f32[8,4,2,512]{3,2,1,0:T(2,128)S(1)}, f32[8,4,2,512]{3,2,1,0:T(2,128)}, u32[]{:S(2)}) copy-start(f32[8,4,2,512]{3,2,1,0:T(2,128)} %param.6) | copy-start | bytes 393220
  16.1 1.6 %copy-start.4 = (f32[512]{0:T(512)S(1)}, f32[512]{0:T(512)}, u32[]{:S(2)}) copy-start(f32[512]{0:T(512)} %param.11) | copy-start | bytes 6148
  16.1 1.5 %copy-start.5 = (f32[512]{0:T(512)S(1)}, f32[512]{0:T(512)}, u32[]{:S(2)}) copy-start(f32[512]{0:T(512)} %param.10) | copy-start | bytes 6148
  26.9 6.1 %collective-permute-start.2 = (f32[8,1,2,512]{3,2,1,0:T(2,128)S(1)}, f32[8,1,2,512]{3,2,1,0:T(2,128)S(1)}, u32[]{:S(2)}, u32[]{:S(2)}) collective-permute-start(f32[8,1,2,512]{3,2,1,0:T(2,128)S(1)} %get-tuple-element.24), channel_id=1, source_target_pairs={{0,1},{2,3},{4,5},{6,7},{8,9},{10,11},{12,13},{14,15},{16,17},{18,... | collective-permute-start | bytes 98312 | tf_op jit(solution)/shard_map/ppermute | solution.py:16
  31.4 5.8 %collective-permute-start.3 = (f32[8,1,2,512]{3,2,1,0:T(2,128)S(1)}, f32[8,1,2,512]{3,2,1,0:T(2,128)S(1)}, u32[]{:S(2)}, u32[]{:S(2)}) collective-permute-start(f32[8,1,2,512]{3,2,1,0:T(2,128)S(1)} %get-tuple-element.25), channel_id=1, source_target_pairs={{1,0},{3,2},{5,4},{7,6},{9,8},{11,10},{13,12},{15,14},{17,16},{19,... | collective-permute-start | bytes 98312 | tf_op jit(solution)/shard_map/ppermute | solution.py:17
  84.9 3.8 %collective-permute-start.4 = (f32[8,1,2,512]{3,2,1,0:T(2,128)S(1)}, f32[8,1,2,512]{3,2,1,0:T(2,128)S(1)}, u32[]{:S(2)}, u32[]{:S(2)}) collective-permute-start(f32[8,1,2,512]{3,2,1,0:T(2,128)S(1)} %get-tuple-element.22), channel_id=1, source_target_pairs={{0,1},{2,3},{4,5},{6,7},{8,9},{10,11},{12,13},{14,15},{16,17},{18,... | collective-permute-start | bytes 98312 | tf_op jit(solution)/shard_map/ppermute | solution.py:16
  87.1 5.8 %collective-permute-start.5 = (f32[8,1,2,512]{3,2,1,0:T(2,128)S(1)}, f32[8,1,2,512]{3,2,1,0:T(2,128)S(1)}, u32[]{:S(2)}, u32[]{:S(2)}) collective-permute-start(f32[8,1,2,512]{3,2,1,0:T(2,128)S(1)} %get-tuple-element.23), channel_id=1, source_target_pairs={{1,0},{3,2},{5,4},{7,6},{9,8},{11,10},{13,12},{15,14},{17,16},{19,... | collective-permute-start | bytes 98312 | tf_op jit(solution)/shard_map/ppermute | solution.py:17
